TPU v7x, 128 devices: a whole 4x4x4 slice. The times are simulated.
128 devices in a mesh: seq: 16 (over z, y_hi, core), tensor: 8 (over x, y_lo).
Axes of the slice: x: 4, y: 4 (y_hi: 2, y_lo: 2; y = y_hi * 2 + y_lo), z: 4, core: 2. Of those that a mesh axis runs over, the one named last changes fastest.
Arguments:
- queries: bfloat16 [3, 48, 40, 5120], P(None, 'seq', None, 'tensor'), may hold values from -16 to 16
- keys_values: bfloat16 [2, 3, 48, 40, 5120], P(None, None, 'seq', None, 'tensor'), may hold values from -16 to 16
- out_weight: bfloat16 [5120, 5120], P('tensor'), may hold values from -0.078125 to 0.078125
- grad_out: bfloat16 [3, 48, 40, 5120], P(None, 'seq', 'tensor'), may hold values from -6 to 6
- window: int32 [40, 3], P('tensor'), may hold values from 0 to 3, as said below
- block_mask: int32 [1, 16, 5, 63], replicated, may hold values from 0 to 1, as said below
Outputs:
- layer_out: bfloat16 [3, 48, 40, 5120], P(None, 'seq', 'tensor')
- grad_queries: bfloat16 [3, 48, 40, 5120], P(None, 'seq', None, 'tensor')
- grad_keys_values: bfloat16 [2, 3, 48, 40, 5120], P(None, None, 'seq', None, 'tensor')
- grad_weight: bfloat16 [5120, 5120], P('tensor', 'seq')
Inputs may be any that keep to these rules, and one draw needn't show every extreme that they name: `window`: in every group of 5 consecutive heads one head has the reach (1, 1, 3). `block_mask`: the middle entry of every tile's row (the tile itself) is 1.
All inputs are finite; a program needn't handle non-finite values.
Results may differ from a plain program's by a relative error of at most 0.014.
Values may be sent and summed in bfloat16 or wider, within the bound.
No kernel may reach another device: no remote copies, remote signals or barrier semaphores. Data moves between devices by JAX's collectives and lax.ppermute only.
A program may use at most 128 MiB of HBM per device.

v0:
```python
import jax
import jax.numpy as jnp
from jax import lax
from jax.sharding import PartitionSpec as P

HEAD_DIM = 128
TILE_F = 3
TILE_H = 3
TILE_W = 8
REACH_F = 1
REACH_H = 1
REACH_W = 3
OFFSETS = 63


def padded(cells, sides, width):
    for axis, dim in sides:
        count = lax.axis_size(axis)
        ends = count - 1
        head = lax.slice_in_dim(cells, 0, width, axis=dim)
        tail = lax.slice_in_dim(cells, cells.shape[dim] - width, cells.shape[dim], axis=dim)
        cells = jnp.concatenate(
            [
                lax.ppermute(tail, axis, [(i, (i + 1) % count) for i in range(ends)]),
                cells,
                lax.ppermute(head, axis, [((i + 1) % count, i) for i in range(ends)]),
            ],
            axis=dim,
        )
    return cells


def from_behind(value, axis, steps):
    count = lax.axis_size(axis)
    initial, last = (max(0, -steps), min(count, count - steps))
    return lax.ppermute(value, axis, [(source, source + steps) for source in range(initial, last)])


def tile_order(grid):
    frames, height, columns, channels = grid.shape
    shaped = grid.reshape(
        frames // TILE_F, TILE_F, height // TILE_H, TILE_H, columns // TILE_W, TILE_W, channels
    )
    return shaped.transpose(0, 2, 4, 1, 3, 5, 6).reshape(-1, channels)


def grid_order(flat_rows, frames, height, columns):
    channels = flat_rows.shape[-1]
    shaped = flat_rows.reshape(
        frames // TILE_F, height // TILE_H, columns // TILE_W, TILE_F, TILE_H, TILE_W, channels
    )
    return shaped.transpose(0, 3, 1, 4, 2, 5, 6).reshape(frames, height, columns, channels)


def tile_coords(frames, height, columns, first_row):
    frame_count = frames // TILE_F
    row_count = height // TILE_H
    column_count = columns // TILE_W
    linear = jnp.arange(frame_count * row_count * column_count, dtype=jnp.int32)
    return (
        linear // (row_count * column_count),
        linear // column_count % row_count + first_row,
        linear % column_count,
    )


def allowed_mask(reach_row, mask_rows, query_tiles, key_tiles, row_tiles):
    delta_f = key_tiles[0][None, :] - query_tiles[0][:, None]
    delta_h = key_tiles[1][None, :] - query_tiles[1][:, None]
    delta_w = key_tiles[2][None, :] - query_tiles[2][:, None]
    inside = (
        (jnp.abs(delta_f) <= reach_row[0])
        & (jnp.abs(delta_h) <= reach_row[1])
        & (jnp.abs(delta_w) <= reach_row[2])
    )
    inside = inside & ((key_tiles[1] >= 0) & (key_tiles[1] < row_tiles))[None, :]
    offset = (
        ((delta_f + REACH_F) * (2 * REACH_H + 1) + delta_h + REACH_H) * (2 * REACH_W + 1)
        + delta_w
        + REACH_W
    )
    mask_bits = jnp.sum(
        jnp.where(
            offset[:, :, None] == jnp.arange(OFFSETS, dtype=jnp.int32), mask_rows[:, None, :], 0
        ),
        axis=-1,
    )
    tiles_ok = inside & (mask_bits > 0)
    tile_size = TILE_F * TILE_H * TILE_W
    query_count, key_count = tiles_ok.shape
    spread = jnp.broadcast_to(
        tiles_ok[:, None, :, None], (query_count, tile_size, key_count, tile_size)
    )
    return spread.reshape(query_count * tile_size, key_count * tile_size)


def split_heads(flat_rows):
    return flat_rows.reshape(flat_rows.shape[0], -1, HEAD_DIM).transpose(1, 0, 2)


def join_heads(stacked):
    return stacked.transpose(1, 0, 2).reshape(stacked.shape[1], -1)


def head_forward(q_rows, k_rows, v_rows, allowed):
    scores = jnp.dot(q_rows, k_rows.T, preferred_element_type=jnp.float32) * HEAD_DIM ** (-0.5)
    scores = jnp.where(allowed, scores, -jnp.inf)
    row_max = jnp.max(scores, axis=1)
    weights = jnp.exp(scores - row_max[:, None])
    row_sum = jnp.sum(weights, axis=1)
    probs = weights / row_sum[:, None]
    attended = jnp.dot(
        probs.astype(jnp.bfloat16), v_rows, preferred_element_type=jnp.float32
    ).astype(jnp.bfloat16)
    return (attended, row_max, row_sum)


def head_backward(q_rows, k_rows, v_rows, grad_rows, allowed, row_max, row_sum, row_delta):
    scores = jnp.dot(q_rows, k_rows.T, preferred_element_type=jnp.float32) * HEAD_DIM ** (-0.5)
    scores = jnp.where(allowed, scores, -jnp.inf)
    probs = jnp.exp(scores - row_max[:, None]) / jnp.maximum(row_sum, 1.0)[:, None]
    rounded = probs.astype(jnp.bfloat16)
    grad_values = jnp.dot(rounded.T, grad_rows, preferred_element_type=jnp.float32)
    grad_probs = jnp.dot(grad_rows, v_rows.T, preferred_element_type=jnp.float32)
    row_delta = jnp.sum(probs * grad_probs, axis=1)
    grad_scores = (probs * (grad_probs - row_delta[:, None]) * HEAD_DIM ** (-0.5)).astype(
        jnp.bfloat16
    )
    grad_queries = jnp.dot(grad_scores, k_rows, preferred_element_type=jnp.float32)
    grad_keys = jnp.dot(grad_scores.T, q_rows, preferred_element_type=jnp.float32)
    return (grad_queries, grad_keys, grad_values, row_delta)


def shards(queries, keys_values, out_weight, grad_out, window, block_mask):
    frames, tile_rows, columns, channels = queries.shape
    model_width = grad_out.shape[3]
    local_columns = grad_out.shape[2]
    row_tiles = lax.axis_size("seq")
    seq_place = lax.axis_index("seq")
    padded_kv = padded(keys_values, (("seq", 2),), TILE_H)
    own_tiles = tile_coords(frames, tile_rows, columns, seq_place)
    wide_tiles = tile_coords(frames, 3 * tile_rows, columns, seq_place - 1)
    own_mask = lax.dynamic_slice_in_dim(block_mask, seq_place, 1, 1).reshape(-1, OFFSETS)
    q_heads = split_heads(tile_order(queries))
    k_heads = split_heads(tile_order(padded_kv[0]))
    v_heads = split_heads(tile_order(padded_kv[1]))

    def forward_one(inputs):
        q_rows, k_rows, v_rows, reach_row = inputs
        allowed = allowed_mask(reach_row, own_mask, own_tiles, wide_tiles, row_tiles)
        return head_forward(q_rows, k_rows, v_rows, allowed)

    attended, row_max, row_sum = lax.map(forward_one, (q_heads, k_heads, v_heads, window))
    attn_grid = grid_order(join_heads(attended), frames, tile_rows, columns)
    flat_rows = attn_grid.transpose(2, 0, 1, 3).reshape(-1, channels)
    mixed_sum = lax.psum_scatter(
        jnp.dot(flat_rows, out_weight, preferred_element_type=jnp.float32)
        .reshape(local_columns * lax.axis_size("tensor"), frames, tile_rows, model_width)
        .astype(jnp.bfloat16),
        "tensor",
        scatter_dimension=0,
        tiled=True,
    ).astype(jnp.float32)
    layer_out = mixed_sum.transpose(1, 2, 0, 3).astype(jnp.bfloat16)
    pieces = lax.all_gather(grad_out, "tensor", axis=2, tiled=True)
    amount = pieces.shape[2]
    flat_piece = pieces.reshape(-1, model_width)
    partial_value = jnp.dot(flat_piece, out_weight.T, preferred_element_type=jnp.float32).astype(
        jnp.bfloat16
    )
    grad_attn = partial_value.reshape(frames, tile_rows, amount, channels)
    used_rows = attn_grid.reshape(-1, channels)
    weight_term = jnp.dot(used_rows.T, flat_piece, preferred_element_type=jnp.float32)
    grad_attn, weight_term = (grad_attn, weight_term)
    grad_weight = lax.psum_scatter(
        weight_term.astype(jnp.bfloat16), "seq", scatter_dimension=1, tiled=True
    )
    g_heads = split_heads(tile_order(grad_attn))

    def backward_one(inputs):
        q_rows, k_rows, v_rows, grad_rows, reach_row, head_max, head_sum = inputs
        allowed = allowed_mask(reach_row, own_mask, own_tiles, wide_tiles, row_tiles)
        result = head_backward(q_rows, k_rows, v_rows, grad_rows, allowed, head_max, head_sum, None)
        return (result[0], result[1], result[2])

    grad_q, grad_k, grad_v = lax.map(
        backward_one, (q_heads, k_heads, v_heads, g_heads, window, row_max, row_sum)
    )
    wide_grads = jnp.stack(
        [
            grid_order(join_heads(grad_k), frames, 3 * tile_rows, columns),
            grid_order(join_heads(grad_v), frames, 3 * tile_rows, columns),
        ]
    )
    from_below = from_behind(wide_grads[:, :, :tile_rows].astype(jnp.bfloat16), "seq", -1).astype(
        jnp.float32
    )
    from_above = from_behind(
        wide_grads[:, :, 2 * tile_rows :].astype(jnp.bfloat16), "seq", 1
    ).astype(jnp.float32)
    grad_kv = (wide_grads[:, :, tile_rows : 2 * tile_rows] + from_below + from_above).astype(
        jnp.bfloat16
    )
    grad_queries = grid_order(join_heads(grad_q), frames, tile_rows, columns).astype(jnp.bfloat16)
    return (layer_out, grad_queries, grad_kv, grad_weight)


def solution(mesh):
    return jax.shard_map(
        shards,
        mesh=mesh,
        in_specs=(
            P(None, "seq", None, "tensor"),
            P(None, None, "seq", None, "tensor"),
            P("tensor", None),
            P(None, "seq", "tensor", None),
            P("tensor", None),
            P(),
        ),
        out_specs=(
            P(None, "seq", "tensor", None),
            P(None, "seq", None, "tensor"),
            P(None, None, "seq", None, "tensor"),
            P("tensor", "seq"),
        ),
        check_vma=False,
    )
```

profile of v0, /device:TPU:0, one launch (start us, length us, event | category | flops | bytes accessed | tf_op | source)
XLA Modules:
  0.0 469.2 jit_solution(18415698256053256040)
XLA Ops:
  7.2 2.4 collective-permute-start
  10.9 2.1 copy.88
  20.9 3.2 reshape_reshape.29
  25.4 3.2 reshape_reshape.30
  29.9 47.5 %while.32 = (s32[]{:T(128)}, bf16[5,360,128]{2,1,0:T(8,128)(2,1)}, f32[5,360]{1,0:T(8,128)S(1)}, f32[5,360]{1,0:T(8,128)S(1)}, s32[5,3]{0,1:T(4,128)S(1)}, /*ind...) while((s32[]{:T(128)}, bf16[5,360,128]{2,1,0:T(8,128)(2,1)}, ...), condition=%wide.region_4.5_spmd.clone.clone, body=%wide.region_0.4_spmd.clone.clone.sunk | while | flops 202237504 | bytes 7008191 | solution.py:153
  33.2 1.9 reshape.435
  37.0 2.2 fusion.148
  42.7 1.9 reshape.435
  46.5 2.2 fusion.148
  56.0 2.2 fusion.148
  65.5 2.2 fusion.148
  71.2 1.9 reshape.435
  75.0 2.2 fusion.148
  79.1 5.9 %convolution_convert_fusion.2 = bf16[40,3,3,5120]{3,0,2,1:T(8,128)(2,1)S(1)} fusion(bf16[640,5120]{1,0:T(8,128)(2,1)} %param.12, bf16[1,1,5,3,3,8,640]{6,5,4,3,2,1,0:T(8,128)(2,1)S(1)} %reshape_reshape.31), kind=kOutput, calls=%fused_computation.138 | convolution fusion | flops 2361139200 | bytes 10700800 | tf_op jit(solution)/shard_map/dot_general | solution.py:157
  85.0 5.3 %copy.87 = bf16[40,3,3,5120]{3,2,1,0:T(4,128)(2,1)} copy(bf16[40,3,3,5120]{3,0,2,1:T(8,128)(2,1)S(1)} %convolution_convert_fusion.2) | data formatting | bytes 7372800 | tf_op jit(solution)/shard_map/convert_element_type | solution.py:159
  90.7 31.7 %all-gather.2.cloned.1.call-done = bf16[3,3,40,5120]{3,1,0,2:T(4,128)(2,1)} async-done(((bf16[3,3,5,5120]{3,1,0,2:T(4,128)(2,1)}), bf16[3,3,40,5120]{3,1,0,2:T(4,128)(2,1)}) %all-gather.2.cloned.1.call-update) | async-done | bytes 3686416 | tf_op jit(solution)/shard_map/all_gather | solution.py:165
  122.4 3.8 copy.89
  126.2 6.6 %convolution_convert_fusion.3 = bf16[360,640]{1,0:T(8,128)(2,1)S(1)} fusion(bf16[360,5120]{1,0:T(8,128)(2,1)S(1)} %bitcast.188, bf16[640,5120]{1,0:T(8,128)(2,1)} %param.12), kind=kOutput, calls=%fused_computation.150 | convolution fusion | flops 2359526400 | bytes 10700800 | tf_op jit(solution)/shard_map/dot_general | solution.py:168
  133.5 8.7 %convolution_convert_fusion.1 = bf16[640,5120]{0,1:T(8,128)(2,1)} fusion(bf16[360,640]{1,0:T(8,128)(2,1)S(1)} %bitcast.198, bf16[360,5120]{1,0:T(8,128)(2,1)} %bitcast.189), kind=kOutput, calls=%fused_computation.137 | convolution fusion | flops 2362572800 | bytes 10700800 | tf_op jit(solution)/shard_map/dot_general | solution.py:173
  143.2 64.0 %while.33 = (s32[]{:T(128)}, bf16[5,360,128]{2,1,0:T(8,128)(2,1)S(1)}, f32[5,1080,128]{2,1,0:T(8,128)}, f32[5,1080,128]{2,1,0:T(8,128)}, s32[5,3]{0,1:T(4,128)S(...) while((s32[]{:T(128)}, ...), condition=%wide.region_9.10_spmd.clone.clone, body=%wide.region_6.9_spmd.clone.clone.sunk | while | flops 501956928 | bytes 16065771 | solution.py:186
  207.2 6.3 %copy.99 = f32[1080,5,128]{2,1,0:T(8,128)} copy(f32[1080,5,128]{2,0,1:T(8,128)} %bitcast.192) | data formatting | bytes 5529600 | tf_op jit(solution)/shard_map/transpose | solution.py:102
  213.5 4.8 %reshape_reshape.35 = f32[1,3,5,3,3,8,640]{6,5,4,3,2,1,0:T(8,128)} reshape(f32[1080,5,128]{2,1,0:T(8,128)} %copy.99) | data formatting | bytes 5529600 | tf_op jit(solution)/shard_map/reshape;reshape | solution.py:49
  218.4 2.1 copy.100
  221.0 5.3 %copy.97 = f32[1080,5,128]{2,1,0:T(8,128)} copy(f32[1080,5,128]{2,0,1:T(8,128)S(1)} %bitcast.193) | data formatting | bytes 5529600 | tf_op jit(solution)/shard_map/transpose | solution.py:102
  226.3 4.8 %reshape_reshape.34 = f32[1,3,5,3,3,8,640]{6,5,4,3,2,1,0:T(8,128)} reshape(f32[1080,5,128]{2,1,0:T(8,128)} %copy.97) | data formatting | bytes 5529600 | tf_op jit(solution)/shard_map/reshape;reshape | solution.py:49
  231.1 2.0 copy.98
  237.2 8.0 %collective-permute-start.3 = (bf16[2,3,3,40,640]{4,3,2,1,0:T(8,128)(2,1)}, bf16[2,3,3,40,640]{4,3,2,1,0:T(8,128)(2,1)}, u32[]{:S(2)}, u32[]{:S(2)}) collective-permute-start(bf16[2,3,3,40,640]{4,3,2,1,0:T(8,128)(2,1)} %get-tuple-element.560), channel_id=1, source_target_pairs={{0,8},{8,16},{16,24},{24,32},{32,40},{40,48},{48,56},{56,64},{64,7... | collective-permute-start | bytes 2764808 | tf_op jit(solution)/shard_map/ppermute | solution.py:36
  246.5 108.6 %all-reduce.3.cloned.1.call-done = bf16[40,3,3,5120]{3,2,1,0:T(4,128)(2,1)} async-done(((bf16[40,3,3,5120]{3,2,1,0:T(4,128)(2,1)}), bf16[40,3,3,5120]{3,2,1,0:T(4,128)(2,1)}) %all-reduce.3.cloned.1.call-update) | async-done | bytes 3686416
  358.5 2.3 convert_element_type.57
  360.8 1.9 copy_bitcast_fusion.2
  362.7 3.0 fusion.102
  365.7 97.0 %reduce-scatter.2.cloned.1.call-done = bf16[640,320]{0,1:T(8,128)(2,1)} async-done(((bf16[640,5120]{0,1:T(8,128)(2,1)}), bf16[640,320]{0,1:T(8,128)(2,1)}) %reduce-scatter.2.cloned.1.call-update) | async-done | bytes 409616 | tf_op jit(solution)/shard_map/reduce_scatter | solution.py:175
  (227 shorter events, 118.2 us)
Async XLA Ops:
  7.2 6.7 %copy-start = (bf16[3,3,40,640]{3,2,1,0:T(8,128)(2,1)S(1)}, bf16[3,3,40,640]{3,2,1,0:T(8,128)(2,1)}, u32[]{:S(2)}) copy-start(bf16[3,3,40,640]{3,2,1,0:T(8,128)(2,1)} %param.10) | copy-start | bytes 1382404
  7.2 115.2 %all-gather.2.cloned.1.call-start = ((), (), s32[]{:S(2)}) async-start(), calls=%async_computation.1 | async-start | bytes 5529600 | tf_op jit(solution)/shard_map/all_gather | solution.py:165
  7.2 7.3 %collective-permute-start = (bf16[2,3,3,40,640]{4,3,2,1,0:T(8,128)(2,1)}, bf16[2,3,3,40,640]{4,3,2,1,0:T(8,128)(2,1)}, u32[]{:S(2)}, u32[]{:S(2)}) collective-permute-start(bf16[2,3,3,40,640]{4,3,2,1,0:T(8,128)(2,1)} %param.11), channel_id=1, source_target_pairs={{0,8},{8,16},{16,24},{24,32},{32,40},{40,48},{48,56},{56,64},{64,7... | collective-permute-start | bytes 2764808 | tf_op jit(solution)/shard_map/ppermute | solution.py:24
  9.6 7.3 %collective-permute-start.1 = (bf16[2,3,3,40,640]{4,3,2,1,0:T(8,128)(2,1)}, bf16[2,3,3,40,640]{4,3,2,1,0:T(8,128)(2,1)}, u32[]{:S(2)}, u32[]{:S(2)}) collective-permute-start(bf16[2,3,3,40,640]{4,3,2,1,0:T(8,128)(2,1)} %param.11), channel_id=1, source_target_pairs={{8,0},{16,8},{24,16},{32,24},{40,32},{48,40},{56,48},{64,56},{72,6... | collective-permute-start | bytes 2764808 | tf_op jit(solution)/shard_map/ppermute | solution.py:26
  13.0 342.1 %all-reduce.3.cloned.1.call-start = ((), (), s32[]{:S(2)}) async-start(), calls=%async_computation.3 | async-start | bytes 9830400
  13.9 1.9 copy-start.5
  28.6 1.3 copy-start.9
  90.4 372.3 %reduce-scatter.2.cloned.1.call-start = ((), (), s32[]{:S(2)}) async-start(), calls=%async_computation.2 | async-start | bytes 6963200 | tf_op jit(solution)/shard_map/reduce_scatter | solution.py:175
  126.2 6.7 %copy-start.3 = (bf16[3,3,40,5120]{3,2,1,0:T(8,128)(2,1)}, bf16[3,3,40,5120]{3,2,1,0:T(8,128)(2,1)S(1)}, u32[]{:S(2)}) copy-start(bf16[3,3,40,5120]{3,2,1,0:T(8,128)(2,1)S(1)} %copy.89) | copy-start | bytes 11059204
  142.2 1.0 copy-start.6
  207.2 6.3 %copy-start.7 = (bf16[5,360,128]{2,1,0:T(8,128)(2,1)}, bf16[5,360,128]{2,1,0:T(8,128)(2,1)S(1)}, u32[]{:S(2)}) copy-start(bf16[5,360,128]{2,1,0:T(8,128)(2,1)S(1)} %get-tuple-element.204) | copy-start | bytes 1382404
  218.4 2.6 copy-start.4
  233.0 1.5 copy-start.2
  234.6 10.7 %copy-start.10 = (u32[128]{0:T(128)S(1)}, u32[128]{0:T(128)}, u32[]{:S(2)}) copy-start(u32[128]{0:T(128)} %constant.149) | copy-start | bytes 1540
  234.6 122.9 %copy-start.8 = (bf16[5,360,128]{2,1,0:T(8,128)(2,1)S(1)}, bf16[5,360,128]{2,1,0:T(8,128)(2,1)}, u32[]{:S(2)}) copy-start(bf16[5,360,128]{2,1,0:T(8,128)(2,1)} %copy-done.7) | copy-start | bytes 1382404
  236.0 126.7 %collective-permute-start.2 = (bf16[2,3,3,40,640]{4,3,2,1,0:T(8,128)(2,1)}, bf16[2,3,3,40,640]{4,3,2,1,0:T(8,128)(2,1)}, u32[]{:S(2)}, u32[]{:S(2)}) collective-permute-start(bf16[2,3,3,40,640]{4,3,2,1,0:T(8,128)(2,1)} %get-tuple-element.559), channel_id=1, source_target_pairs={{8,0},{16,8},{24,16},{32,24},{40,32},{48,40},{56,48},{64,56},{72,6... | collective-permute-start | bytes 2764808 | tf_op jit(solution)/shard_map/ppermute | solution.py:36
  237.2 125.4 %collective-permute-start.3 = (bf16[2,3,3,40,640]{4,3,2,1,0:T(8,128)(2,1)}, bf16[2,3,3,40,640]{4,3,2,1,0:T(8,128)(2,1)}, u32[]{:S(2)}, u32[]{:S(2)}) collective-permute-start(bf16[2,3,3,40,640]{4,3,2,1,0:T(8,128)(2,1)} %get-tuple-element.560), channel_id=1, source_target_pairs={{0,8},{8,16},{16,24},{24,32},{32,40},{40,48},{48,56},{56,64},{64,7... | collective-permute-start | bytes 2764808 | tf_op jit(solution)/shard_map/ppermute | solution.py:36
  360.8 101.9 %copy-start.1 = (bf16[3,3,40,640]{3,2,1,0:T(8,128)(2,1)S(1)}, bf16[3,3,40,640]{3,2,1,0:T(8,128)(2,1)}, u32[]{:S(2)}) copy-start(bf16[3,3,40,640]{3,2,1,0:T(8,128)(2,1)} %param.10) | copy-start | bytes 1382404
Sparse Core Ops, SparseCore 0:
  13.2 109.1 all-gather.1
  124.9 230.1 all-reduce.2
  359.9 102.7 reduce-scatter.1
where the time goes:
time: 471 us; the launch traced here: 469 us
  waiting for transfers between devices  238 us (51%)
  local copies, waits for them, and re-layouts  94.9 us (20%)
  matrix products  76.7 us (16%)
  other arithmetic  30.8 us (7%)
  between operations  14.7 us (3%)
  starting transfers between devices  13.3 us (3%)
    unnamed x4, waiting for transfers between devices  109 us
    reduce_scatter x1, waiting for transfers between devices, shards(): lax.psum_scatter(weight_term.astype(jnp.bfloat16), 'seq', scatter_dimensi...  97 us
    all_gather x1, waiting for transfers between devices, shards(): pieces = lax.all_gather(grad_out, 'tensor', axis=2, tiled=True)  31.7 us
    reshape x10, local copies, waits for them, and re-layouts, allowed_mask(): return spread.reshape(query_count * tile_size, key_count * tile_size)  18.6 us
    and x10, other arithmetic, allowed_mask(): tiles_ok = inside & (mask_bits > 0)  13.6 us
    transpose x3, local copies, waits for them, and re-layouts, join_heads(): return stacked.transpose(1, 0, 2).reshape(stacked.shape[1], -1)  12.8 us
    dot_general x5, matrix products, head_forward(): jnp.dot(probs.astype(jnp.bfloat16), v_rows, preferred_element_type=jnp.fl...  11.2 us
    unnamed x32, local copies, waits for them, and re-layouts  10.5 us
  transfers between devices with their start and end apart: 7, of which 4 were waited for; matrix products, arithmetic and copies ran while one was open for 43% of the time, Pallas kernels for 0%

commit v1 on v0

--- a/solution.py
+++ b/solution.py
@@ -162,7 +162,9 @@
         tiled=True,
     ).astype(jnp.float32)
     layer_out = mixed_sum.transpose(1, 2, 0, 3).astype(jnp.bfloat16)
-    pieces = lax.all_gather(grad_out, "tensor", axis=2, tiled=True)
+    pieces = jnp.concatenate(
+        lax.all_to_all(jnp.stack([grad_out] * lax.axis_size("tensor")), "tensor", 0, 0), axis=2
+    )
     amount = pieces.shape[2]
     flat_piece = pieces.reshape(-1, model_width)
     partial_value = jnp.dot(flat_piece, out_weight.T, preferred_element_type=jnp.float32).astype(

time: 471 us -> 415 us (0.88); the launches traced: 469 us -> 408 us
  waiting for transfers between devices: 238 us -> 118 us
  starting transfers between devices: 13.3 us -> 55 us
  local copies, waits for them, and re-layouts: 94.9 us -> 110 us
    reduce_scatter x1, waiting for transfers between devices: 97 us -> 0.01 us  [shards(): lax.psum_scatter(weight_term.astype(jnp.bfloat16), 'seq', scatter_dimensi...]
    ppermute x2, starting transfers between devices: 9.29 us -> 45.2 us  [from_behind(): lax.ppermute(value, axis, [(source, source + steps) for source in range(i...]
    all_gather x1 -> x0, waiting for transfers between devices: 31.7 us -> none  [shards(): pieces = lax.all_gather(grad_out, 'tensor', axis=2, tiled=True)]
    another operation x0 -> x2, local copies, waits for them, and re-layouts: none -> 12.5 us  [the longest x1 8.02 us: shards(): flat_piece = pieces.reshape(-1, model_width)]
    unnamed x4 -> x3, waiting for transfers between devices: 109 us -> 118 us
    reshape x0 -> x1, local copies, waits for them, and re-layouts: none -> 6.71 us  [shards(): jnp.concatenate(lax.all_to_all(jnp.stack([grad_out] * lax.axis_size('tens...]
    all_to_all x0 -> x1, starting transfers between devices: none -> 5.87 us  [shards(): lax.all_to_all(jnp.stack([grad_out] * lax.axis_size('tensor')), 'tensor',...]
    unnamed x32 -> x31, local copies, waits for them, and re-layouts: 10.5 us -> 9.06 us
  transfers between devices with their start and end apart: 7 -> 7, of which waited for: 4 -> 1; matrix products, arithmetic and copies ran while one was open for 43% -> 53% of each run, Pallas kernels for 0% -> 0%
where the time goes in v1:
time: 415 us; the launch traced here: 408 us
  waiting for transfers between devices  118 us (28%)
  local copies, waits for them, and re-layouts  110 us (27%)
  matrix products  77.3 us (19%)
  starting transfers between devices  55 us (13%)
  other arithmetic  30.5 us (7%)
  between operations  16.7 us (4%)
    unnamed x3, waiting for transfers between devices  118 us
    ppermute x2, starting transfers between devices, from_behind(): lax.ppermute(value, axis, [(source, source + steps) for source in range(i...  45.2 us
    reshape x10, local copies, waits for them, and re-layouts, allowed_mask(): return spread.reshape(query_count * tile_size, key_count * tile_size)  18.6 us
    and x10, other arithmetic, allowed_mask(): tiles_ok = inside & (mask_bits > 0)  13.1 us
    transpose x3, local copies, waits for them, and re-layouts, join_heads(): return stacked.transpose(1, 0, 2).reshape(stacked.shape[1], -1)  12.9 us
    dot_general x5, matrix products, head_forward(): jnp.dot(probs.astype(jnp.bfloat16), v_rows, preferred_element_type=jnp.fl...  11.2 us
    another operation x3, local copies, waits for them, and re-layouts, grid_order(): flat_rows.reshape(frames // TILE_F, height // TILE_H, columns // TILE_W,...  10.3 us
    dot_general x5, matrix products, head_backward(): jnp.dot(q_rows, k_rows.T, preferred_element_type=jnp.float32)  9.48 us
  transfers between devices with their start and end apart: 7, of which 1 were waited for; matrix products, arithmetic and copies ran while one was open for 53% of the time, Pallas kernels for 0%

profile of v1, /device:TPU:0, one launch (start us, length us, event | category | flops | bytes accessed | tf_op | source)
XLA Modules:
  0.0 408.5 jit_solution(12369043092797388487)
XLA Ops:
  8.0 2.4 collective-permute-start
  11.7 4.5 %stack.4 = bf16[8,3,3,5,5120]{4,2,3,1,0:T(4,128)(2,1)} broadcast(bf16[3,3,5,5120]{3,1,2,0:T(4,128)(2,1)} %param.13), dimensions={1,2,3,4} | broadcast | bytes 4147200 | tf_op jit(solution)/shard_map/stack | solution.py:166
  16.2 5.9 %all-to-all-start = ((bf16[8,3,3,5,5120]{4,2,3,1,0:T(4,128)(2,1)}), bf16[8,3,3,5,5120]{4,2,3,1,0:T(4,128)(2,1)}, u32[]{:S(2)}, u32[]{:S(2)}) async-start(bf16[8,3,3,5,5120]{4,2,3,1,0:T(4,128)(2,1)} %stack.4), calls=%async_computation | async-start | bytes 9830400 | tf_op jit(solution)/shard_map/all_to_all | solution.py:166
  29.0 3.6 reshape_reshape.32
  35.7 3.2 reshape_reshape.33
  40.2 46.8 %while.32 = (s32[]{:T(128)}, bf16[5,360,128]{2,1,0:T(8,128)(2,1)}, f32[5,360]{1,0:T(8,128)S(1)}, f32[5,360]{1,0:T(8,128)S(1)}, s32[5,3]{0,1:T(4,128)S(1)}, /*ind...) while((s32[]{:T(128)}, bf16[5,360,128]{2,1,0:T(8,128)(2,1)}, ...), condition=%wide.region_4.5_spmd.clone.clone, body=%wide.region_0.4_spmd.clone.clone.sunk | while | flops 202237504 | bytes 7008183 | solution.py:153
  47.2 2.2 fusion.148
  56.6 2.2 fusion.148
  66.0 2.2 fusion.148
  75.3 2.2 fusion.148
  84.7 2.2 fusion.148
  88.8 5.9 %convolution_convert_fusion.2 = bf16[40,3,3,5120]{3,0,2,1:T(8,128)(2,1)S(1)} fusion(bf16[640,5120]{1,0:T(8,128)(2,1)} %param.12, bf16[1,1,5,3,3,8,640]{6,5,4,3,2,1,0:T(8,128)(2,1)S(1)} %reshape_reshape.34), kind=kOutput, calls=%fused_computation.138 | convolution fusion | flops 2361139200 | bytes 10700800 | tf_op jit(solution)/shard_map/dot_general | solution.py:157
  94.7 5.3 %copy.87 = bf16[40,3,3,5120]{3,2,1,0:T(4,128)(2,1)} copy(bf16[40,3,3,5120]{3,0,2,1:T(8,128)(2,1)S(1)} %convolution_convert_fusion.2) | data formatting | bytes 7372800 | tf_op jit(solution)/shard_map/convert_element_type | solution.py:159
  100.3 6.7 %copy.88 = bf16[3,3,8,5,5120]{4,3,2,1,0:T(8,128)(2,1)} copy(bf16[3,3,8,5,5120]{4,1,3,0,2:T(4,128)(2,1)} %bitcast.16) | data formatting | bytes 7372800 | tf_op jit(solution)/shard_map/reshape | solution.py:165
  107.1 8.0 %reshape_reshape.35 = bf16[360,5120]{1,0:T(8,128)(2,1)} reshape(bf16[3,3,8,5,5120]{4,3,2,1,0:T(8,128)(2,1)} %copy.88) | data formatting | bytes 7372800 | tf_op jit(solution)/shard_map/reshape;reshape | solution.py:169
  115.1 7.0 %convolution_convert_fusion.3 = bf16[360,640]{1,0:T(8,128)(2,1)S(1)} fusion(bf16[360,5120]{1,0:T(8,128)(2,1)} %reshape_reshape.35, bf16[640,5120]{1,0:T(8,128)(2,1)} %param.12), kind=kOutput, calls=%fused_computation.150 | convolution fusion | flops 2359526400 | bytes 10700800 | tf_op jit(solution)/shard_map/dot_general | solution.py:170
  122.8 8.7 %convolution_convert_fusion.1 = bf16[640,5120]{0,1:T(8,128)(2,1)} fusion(bf16[360,640]{1,0:T(8,128)(2,1)S(1)} %bitcast.196, bf16[360,5120]{1,0:T(8,128)(2,1)} %reshape_reshape.35), kind=kOutput, calls=%fused_computation.137 | convolution fusion | flops 2362572800 | bytes 10700800 | tf_op jit(solution)/shard_map/dot_general | solution.py:175
  132.5 65.0 %while.33 = (s32[]{:T(128)}, bf16[5,360,128]{2,1,0:T(8,128)(2,1)S(1)}, f32[5,1080,128]{2,1,0:T(8,128)}, f32[5,1080,128]{2,1,0:T(8,128)}, s32[5,3]{0,1:T(4,128)S(...) while((s32[]{:T(128)}, ...), condition=%wide.region_9.10_spmd.clone.clone, body=%wide.region_6.9_spmd.clone.clone.sunk | while | flops 501956928 | bytes 16065763 | solution.py:188
  139.4 1.9 multiply_reduce_fusion.2
  152.3 1.9 multiply_reduce_fusion.2
  165.4 1.9 multiply_reduce_fusion.2
  178.3 1.9 multiply_reduce_fusion.2
  191.3 1.9 multiply_reduce_fusion.2
  197.6 6.4 %copy.96 = f32[1080,5,128]{2,1,0:T(8,128)} copy(f32[1080,5,128]{2,0,1:T(8,128)} %bitcast.190) | data formatting | bytes 5529600 | tf_op jit(solution)/shard_map/transpose | solution.py:102
  204.0 5.0 %reshape_reshape.38 = f32[1,3,5,3,3,8,640]{6,5,4,3,2,1,0:T(8,128)} reshape(f32[1080,5,128]{2,1,0:T(8,128)} %copy.96) | data formatting | bytes 5529600 | tf_op jit(solution)/shard_map/reshape;reshape | solution.py:49
  209.0 2.3 copy.97
  211.9 5.3 %copy.98 = f32[1080,5,128]{2,1,0:T(8,128)} copy(f32[1080,5,128]{2,0,1:T(8,128)S(1)} %bitcast.191) | data formatting | bytes 5529600 | tf_op jit(solution)/shard_map/transpose | solution.py:102
  217.2 4.8 %reshape_reshape.39 = f32[1,3,5,3,3,8,640]{6,5,4,3,2,1,0:T(8,128)} reshape(f32[1080,5,128]{2,1,0:T(8,128)} %copy.98) | data formatting | bytes 5529600 | tf_op jit(solution)/shard_map/reshape;reshape | solution.py:49
  222.0 2.5 copy.99
  228.8 43.9 %collective-permute-start.3 = (bf16[2,3,3,40,640]{4,3,2,1,0:T(8,128)(2,1)}, bf16[2,3,3,40,640]{4,3,2,1,0:T(8,128)(2,1)}, u32[]{:S(2)}, u32[]{:S(2)}) collective-permute-start(bf16[2,3,3,40,640]{4,3,2,1,0:T(8,128)(2,1)} %get-tuple-element.560), channel_id=1, source_target_pairs={{0,8},{8,16},{16,24},{24,32},{32,40},{40,48},{48,56},{56,64},{64,7... | collective-permute-start | bytes 2764808 | tf_op jit(solution)/shard_map/ppermute | solution.py:36
  277.5 3.1 fusion.102
  280.5 117.9 %all-reduce.3.cloned.1.call-done = bf16[40,3,3,5120]{3,2,1,0:T(4,128)(2,1)} async-done(((bf16[40,3,3,5120]{3,2,1,0:T(4,128)(2,1)}), bf16[40,3,3,5120]{3,2,1,0:T(4,128)(2,1)}) %all-reduce.3.cloned.1.call-update) | async-done | bytes 3686416
  (227 shorter events, 117.8 us)
Async XLA Ops:
  8.0 14.9 %copy-start = (bf16[3,3,40,640]{3,2,1,0:T(8,128)(2,1)S(1)}, bf16[3,3,40,640]{3,2,1,0:T(8,128)(2,1)}, u32[]{:S(2)}) copy-start(bf16[3,3,40,640]{3,2,1,0:T(8,128)(2,1)} %param.10) | copy-start | bytes 1382404
  8.0 15.6 %collective-permute-start = (bf16[2,3,3,40,640]{4,3,2,1,0:T(8,128)(2,1)}, bf16[2,3,3,40,640]{4,3,2,1,0:T(8,128)(2,1)}, u32[]{:S(2)}, u32[]{:S(2)}) collective-permute-start(bf16[2,3,3,40,640]{4,3,2,1,0:T(8,128)(2,1)} %param.11), channel_id=1, source_target_pairs={{0,8},{8,16},{16,24},{24,32},{32,40},{40,48},{48,56},{56,64},{64,7... | collective-permute-start | bytes 2764808 | tf_op jit(solution)/shard_map/ppermute | solution.py:24
  10.4 14.6 %collective-permute-start.1 = (bf16[2,3,3,40,640]{4,3,2,1,0:T(8,128)(2,1)}, bf16[2,3,3,40,640]{4,3,2,1,0:T(8,128)(2,1)}, u32[]{:S(2)}, u32[]{:S(2)}) collective-permute-start(bf16[2,3,3,40,640]{4,3,2,1,0:T(8,128)(2,1)} %param.11), channel_id=1, source_target_pairs={{8,0},{16,8},{24,16},{32,24},{40,32},{48,40},{56,48},{64,56},{72,6... | collective-permute-start | bytes 2764808 | tf_op jit(solution)/shard_map/ppermute | solution.py:26
  16.2 84.1 %all-to-all-start = ((bf16[8,3,3,5,5120]{4,2,3,1,0:T(4,128)(2,1)}), bf16[8,3,3,5,5120]{4,2,3,1,0:T(4,128)(2,1)}, u32[]{:S(2)}, u32[]{:S(2)}) async-start(bf16[8,3,3,5,5120]{4,2,3,1,0:T(4,128)(2,1)} %stack.4), calls=%async_computation | async-start | bytes 9830400 | tf_op jit(solution)/shard_map/all_to_all | solution.py:166
  22.1 376.4 %all-reduce.3.cloned.1.call-start = ((), (), s32[]{:S(2)}) async-start(), calls=%async_computation.3 | async-start | bytes 9830400
  23.0 1.9 copy-start.5
  32.6 1.8 copy-start.3
  38.9 1.3 copy-start.9
  100.0 300.8 %reduce-scatter.2.cloned.1.call-start = ((), (), s32[]{:S(2)}) async-start(), calls=%async_computation.2 | async-start | bytes 6963200 | tf_op jit(solution)/shard_map/reduce_scatter | solution.py:177
  131.5 1.0 copy-start.6
  197.6 6.4 %copy-start.7 = (bf16[5,360,128]{2,1,0:T(8,128)(2,1)}, bf16[5,360,128]{2,1,0:T(8,128)(2,1)S(1)}, u32[]{:S(2)}) copy-start(bf16[5,360,128]{2,1,0:T(8,128)(2,1)S(1)} %get-tuple-element.204) | copy-start | bytes 1382404
  209.0 2.9 copy-start.4
  224.5 1.5 copy-start.2
  226.1 46.6 %copy-start.10 = (u32[128]{0:T(128)S(1)}, u32[128]{0:T(128)}, u32[]{:S(2)}) copy-start(u32[128]{0:T(128)} %constant.149) | copy-start | bytes 1540
  226.1 47.9 %copy-start.8 = (bf16[5,360,128]{2,1,0:T(8,128)(2,1)S(1)}, bf16[5,360,128]{2,1,0:T(8,128)(2,1)}, u32[]{:S(2)}) copy-start(bf16[5,360,128]{2,1,0:T(8,128)(2,1)} %copy-done.7) | copy-start | bytes 1382404
  227.5 50.0 %collective-permute-start.2 = (bf16[2,3,3,40,640]{4,3,2,1,0:T(8,128)(2,1)}, bf16[2,3,3,40,640]{4,3,2,1,0:T(8,128)(2,1)}, u32[]{:S(2)}, u32[]{:S(2)}) collective-permute-start(bf16[2,3,3,40,640]{4,3,2,1,0:T(8,128)(2,1)} %get-tuple-element.559), channel_id=1, source_target_pairs={{8,0},{16,8},{24,16},{32,24},{40,32},{48,40},{56,48},{64,56},{72,6... | collective-permute-start | bytes 2764808 | tf_op jit(solution)/shard_map/ppermute | solution.py:36
  228.8 48.7 %collective-permute-start.3 = (bf16[2,3,3,40,640]{4,3,2,1,0:T(8,128)(2,1)}, bf16[2,3,3,40,640]{4,3,2,1,0:T(8,128)(2,1)}, u32[]{:S(2)}, u32[]{:S(2)}) collective-permute-start(bf16[2,3,3,40,640]{4,3,2,1,0:T(8,128)(2,1)} %get-tuple-element.560), channel_id=1, source_target_pairs={{0,8},{8,16},{16,24},{24,32},{32,40},{40,48},{48,56},{56,64},{64,7... | collective-permute-start | bytes 2764808 | tf_op jit(solution)/shard_map/ppermute | solution.py:36
  277.5 123.3 %copy-start.1 = (bf16[3,3,40,640]{3,2,1,0:T(8,128)(2,1)S(1)}, bf16[3,3,40,640]{3,2,1,0:T(8,128)(2,1)}, u32[]{:S(2)}) copy-start(bf16[3,3,40,640]{3,2,1,0:T(8,128)(2,1)} %param.10) | copy-start | bytes 1382404
Sparse Core Ops, SparseCore 0:
  100.2 298.2 all-reduce.2
Sparse Core Ops, SparseCore 1:
  131.6 164.1 reduce-scatter.1
